TPU v7x, 32 devices: a whole 2x2x4 slice. The times are simulated.
32 devices in a mesh: dp: 16 (over z, y, core), tensor: 2 (over x).
Axes of the slice: x: 2, y: 2, z: 4, core: 2. Of those that a mesh axis runs over, the one named last changes fastest.
Arguments:
- block_input: bfloat16 [160, 197, 768], P('dp'), may hold values from -6 to 6
- image_counts: int32 [16], P('dp'), may hold values from 1 to 10, 88 in all
- first_norm_gain: float32 [768], replicated, may hold values from 0.1 to 1.9
- first_norm_bias: float32 [768], replicated, may hold values from -3 to 3
- w_qkv: bfloat16 [3, 768, 768], P(None, None, 'tensor'), may hold values from -8 to 8
- qv_bias: float32 [2, 768], P(None, 'tensor'), may hold values from -3 to 3
- w_out: bfloat16 [768, 768], P('tensor'), may hold values from -0.75 to 0.75
- b_out: float32 [768], replicated, may hold values from -3 to 3
- second_norm_gain: float32 [768], replicated, may hold values from 0.1 to 1.9
- second_norm_bias: float32 [768], replicated, may hold values from -3 to 3
- w_fc1: bfloat16 [768, 3072], P(None, 'tensor'), may hold values from -0.21875 to 0.21875
- b_fc1: float32 [3072], P('tensor'), may hold values from -3 to 3
- w_fc2: bfloat16 [3072, 768], P('tensor'), may hold values from -0.109375 to 0.109375
- b_fc2: float32 [768], replicated, may hold values from -3 to 3
- cotangent: bfloat16 [160, 197, 768], P('dp'), may hold values from -6 to 6
Outputs:
- block_out: bfloat16 [160, 197, 768], P('dp')
- gradient_of_input: bfloat16 [160, 197, 768], P('dp')
- first_norm_gain_gradient: float32 [768], replicated
- grad_ln1_bias: float32 [768], replicated
- grad_w_qkv: float32 [3, 768, 768], P(None, None, 'tensor')
- grad_qv_bias: float32 [2, 768], P(None, 'tensor')
- grad_w_out: float32 [768, 768], P('tensor')
- grad_b_out: float32 [768], replicated
- second_norm_gain_gradient: float32 [768], replicated
- grad_ln2_bias: float32 [768], replicated
- grad_w_fc1: float32 [768, 3072], P(None, 'tensor')
- grad_b_fc1: float32 [3072], P('tensor')
- grad_w_fc2: float32 [3072, 768], P('tensor')
- grad_b_fc2: float32 [768], replicated
All inputs are finite; a program needn't handle non-finite values. No bound on the sum of `image_counts` on one device may be relied on, other than what follows from the above.
Results may differ from a plain program's by a relative error of at most 0.012.
The roundings to bfloat16 on the way count: a program that leaves them out, or rounds other values in their place, can miss the bound.
Values sent between devices are 32-bit elements; how exact they have to be, the bound alone decides.
No kernel may reach another device: no remote copies, remote signals or barrier semaphores. Data moves between devices by JAX's collectives and lax.ppermute only.
A program may use at most 256 MiB of HBM per device.

v0:
```python
import jax
import jax.numpy as jnp
from jax import lax
from jax.sharding import PartitionSpec as P

HD = 64
EPSILON = 1e-06
INV_ROOT2 = 0.7071067811865476
INV_ROOT2PI = 0.3989422804014327


def apply_layer_norm(values, norm_gain, norm_bias):
    center = jnp.mean(values, -1, keepdims=True)
    shifted = values - center
    spread = jnp.mean(shifted * shifted, -1, keepdims=True)
    inv_std = lax.rsqrt(spread + EPSILON)
    normed = shifted * inv_std
    return (normed * norm_gain + norm_bias, normed, inv_std)


def norm_backward_pass(grad_normed, normed, inv_std, norm_gain):
    scaled = grad_normed * norm_gain
    first = jnp.mean(scaled, -1, keepdims=True)
    second = jnp.mean(scaled * normed, -1, keepdims=True)
    return inv_std * (scaled - first - normed * second)


def gelu_value(pre_act):
    return 0.5 * pre_act * (1.0 + lax.erf(pre_act * INV_ROOT2))


def gelu_slope(pre_act):
    return (
        0.5 * (1.0 + lax.erf(pre_act * INV_ROOT2))
        + pre_act * jnp.exp(-0.5 * pre_act * pre_act) * INV_ROOT2PI
    )


def head_scores(queries, keys_all, scale):
    return (
        jnp.einsum("ishd,ithd->ihst", queries, keys_all, preferred_element_type=jnp.float32) * scale
    )


def shards(
    block_input,
    image_counts,
    first_norm_gain,
    first_norm_bias,
    w_qkv,
    qv_bias,
    w_out,
    b_out,
    second_norm_gain,
    second_norm_bias,
    w_fc1,
    b_fc1,
    w_fc2,
    b_fc2,
    cotangent,
):
    float_thirtytwo = jnp.float32
    bfloat_sixteen = jnp.bfloat16
    image_batch, sequence_length, model_width = block_input.shape
    total_rows = image_batch * sequence_length
    local_heads = w_qkv.shape[2] // HD
    local_width = local_heads * HD
    scale = HD ** (-0.5)
    shape4 = (image_batch, sequence_length, local_heads, HD)
    live_rows = (jnp.arange(total_rows, dtype=jnp.int32) // sequence_length < image_counts[0])[
        :, None
    ]
    input_tokens = block_input.reshape(total_rows, model_width).astype(float_thirtytwo)
    first_normed_tokens, first_centered_scaled, first_inverse_deviation = apply_layer_norm(
        input_tokens, first_norm_gain, first_norm_bias
    )
    normed_one_b = first_normed_tokens.astype(bfloat_sixteen)
    projected = jnp.einsum(
        "nd,cde->cne", normed_one_b, w_qkv, preferred_element_type=float_thirtytwo
    )
    queries = (projected[0] + qv_bias[0]).astype(bfloat_sixteen).reshape(shape4)
    keys_all = projected[1].astype(bfloat_sixteen).reshape(shape4)
    values_all = (projected[2] + qv_bias[1]).astype(bfloat_sixteen).reshape(shape4)
    scores = head_scores(queries, keys_all, scale)
    log_total = jax.nn.logsumexp(scores, axis=-1)
    probs = jnp.exp(scores - log_total[..., None]).astype(bfloat_sixteen)
    context = (
        jnp.einsum("ihst,ithd->ishd", probs, values_all, preferred_element_type=float_thirtytwo)
        .astype(bfloat_sixteen)
        .reshape(total_rows, local_width)
    )
    attn_part = jnp.dot(context, w_out, preferred_element_type=float_thirtytwo)
    attn_full = lax.psum(attn_part, "tensor")
    residual_stream = input_tokens + (attn_full + b_out)
    second_normed_tokens, second_centered_scaled, second_inverse_deviation = apply_layer_norm(
        residual_stream, second_norm_gain, second_norm_bias
    )
    normed_two_b = second_normed_tokens.astype(bfloat_sixteen)
    pre_act = jnp.dot(normed_two_b, w_fc1, preferred_element_type=float_thirtytwo) + b_fc1
    activated = gelu_value(pre_act).astype(bfloat_sixteen)
    mlp_part = jnp.dot(activated, w_fc2, preferred_element_type=float_thirtytwo)
    mlp_full = lax.psum(mlp_part, "tensor")
    outputs = residual_stream + (mlp_full + b_fc2)
    block_out = (
        jnp.where(live_rows, outputs, 0.0)
        .astype(bfloat_sixteen)
        .reshape(image_batch, sequence_length, model_width)
    )
    output_gradient = jnp.where(
        live_rows, cotangent.reshape(total_rows, model_width), jnp.zeros((), bfloat_sixteen)
    )
    grad_w_fc2 = jnp.einsum(
        "nf,nd->fd", activated, output_gradient, preferred_element_type=float_thirtytwo
    )
    grad_b_fc2 = jnp.sum(output_gradient.astype(float_thirtytwo), axis=0)
    grad_act = jnp.einsum(
        "nd,fd->nf", output_gradient, w_fc2, preferred_element_type=float_thirtytwo
    )
    grad_pre = (grad_act * gelu_slope(pre_act)).astype(bfloat_sixteen)
    grad_w_fc1 = jnp.einsum(
        "nd,nf->df", normed_two_b, grad_pre, preferred_element_type=float_thirtytwo
    )
    grad_b_fc1 = jnp.sum(grad_pre.astype(float_thirtytwo), axis=0)
    norm_two_part = jnp.einsum("nf,df->nd", grad_pre, w_fc1, preferred_element_type=float_thirtytwo)
    second_normed_gradient = lax.psum(norm_two_part, "tensor")
    second_norm_gain_gradient = jnp.sum(second_normed_gradient * second_centered_scaled, axis=0)
    grad_ln2_bias = jnp.sum(second_normed_gradient, axis=0)
    residual_gradient = output_gradient.astype(float_thirtytwo) + norm_backward_pass(
        second_normed_gradient, second_centered_scaled, second_inverse_deviation, second_norm_gain
    )
    grad_resid_b = residual_gradient.astype(bfloat_sixteen)
    grad_w_out = jnp.einsum(
        "ne,nd->ed", context, grad_resid_b, preferred_element_type=float_thirtytwo
    )
    grad_b_out = jnp.sum(residual_gradient, axis=0)
    grad_context = (
        jnp.einsum("nd,ed->ne", grad_resid_b, w_out, preferred_element_type=float_thirtytwo)
        .astype(bfloat_sixteen)
        .reshape(shape4)
    )
    probs_full = jnp.exp(head_scores(queries, keys_all, scale) - log_total[..., None])
    probs_again = probs_full.astype(bfloat_sixteen)
    grad_values = jnp.einsum(
        "ihst,ishd->ithd", probs_again, grad_context, preferred_element_type=float_thirtytwo
    ).astype(bfloat_sixteen)
    grad_probs = jnp.einsum(
        "ishd,ithd->ihst", grad_context, values_all, preferred_element_type=float_thirtytwo
    )
    row_dot = jnp.sum(probs_full * grad_probs, axis=-1, keepdims=True)
    grad_scores = (probs_full * (grad_probs - row_dot)).astype(bfloat_sixteen)
    grad_queries = (
        jnp.einsum("ihst,ithd->ishd", grad_scores, keys_all, preferred_element_type=float_thirtytwo)
        * scale
    ).astype(bfloat_sixteen)
    grad_keys = (
        jnp.einsum("ihst,ishd->ithd", grad_scores, queries, preferred_element_type=float_thirtytwo)
        * scale
    ).astype(bfloat_sixteen)
    grad_proj = jnp.stack([grad_queries, grad_keys, grad_values]).reshape(
        3, total_rows, local_width
    )
    grad_w_qkv = jnp.einsum(
        "nd,cne->cde", normed_one_b, grad_proj, preferred_element_type=float_thirtytwo
    )
    grad_qv_bias = jnp.stack(
        [
            jnp.sum(grad_proj[0].astype(float_thirtytwo), axis=0),
            jnp.sum(grad_proj[2].astype(float_thirtytwo), axis=0),
        ]
    )
    norm_one_part = jnp.einsum(
        "cne,cde->nd", grad_proj, w_qkv, preferred_element_type=float_thirtytwo
    )
    first_normed_gradient = lax.psum(norm_one_part, "tensor")
    first_norm_gain_gradient = jnp.sum(first_normed_gradient * first_centered_scaled, axis=0)
    grad_ln1_bias = jnp.sum(first_normed_gradient, axis=0)
    gradient_of_input = (
        (
            residual_gradient
            + norm_backward_pass(
                first_normed_gradient,
                first_centered_scaled,
                first_inverse_deviation,
                first_norm_gain,
            )
        )
        .astype(bfloat_sixteen)
        .reshape(image_batch, sequence_length, model_width)
    )
    summed = lax.psum(
        (
            first_norm_gain_gradient,
            grad_ln1_bias,
            grad_w_qkv,
            grad_qv_bias,
            grad_w_out,
            grad_b_out,
            second_norm_gain_gradient,
            grad_ln2_bias,
            grad_w_fc1,
            grad_b_fc1,
            grad_w_fc2,
            grad_b_fc2,
        ),
        "dp",
    )
    first_norm_gain_gradient, grad_ln1_bias, grad_w_qkv, grad_qv_bias, grad_w_out, grad_b_out = (
        summed[0],
        summed[1],
        summed[2],
        summed[3],
        summed[4],
        summed[5],
    )
    second_norm_gain_gradient, grad_ln2_bias, grad_w_fc1, grad_b_fc1, grad_w_fc2, grad_b_fc2 = (
        summed[6],
        summed[7],
        summed[8],
        summed[9],
        summed[10],
        summed[11],
    )
    return (
        block_out,
        gradient_of_input,
        first_norm_gain_gradient,
        grad_ln1_bias,
        grad_w_qkv,
        grad_qv_bias,
        grad_w_out,
        grad_b_out,
        second_norm_gain_gradient,
        grad_ln2_bias,
        grad_w_fc1,
        grad_b_fc1,
        grad_w_fc2,
        grad_b_fc2,
    )


def solution(mesh):
    in_specs = (
        P("dp", None, None),
        P("dp"),
        P(),
        P(),
        P(None, None, "tensor"),
        P(None, "tensor"),
        P("tensor", None),
        P(),
        P(),
        P(),
        P(None, "tensor"),
        P("tensor"),
        P("tensor", None),
        P(),
        P("dp", None, None),
    )
    out_specs = (
        P("dp", None, None),
        P("dp", None, None),
        P(),
        P(),
        P(None, None, "tensor"),
        P(None, "tensor"),
        P("tensor", None),
        P(),
        P(),
        P(),
        P(None, "tensor"),
        P("tensor"),
        P("tensor", None),
        P(),
    )
    return jax.shard_map(shards, mesh=mesh, in_specs=in_specs, out_specs=out_specs, check_vma=False)
```

profile of v0, /device:TPU:0, one launch (start us, length us, event | category | flops | bytes accessed | tf_op | source)
XLA Modules:
  0.0 1190.0 jit_solution(15098997224716500326)
XLA Ops:
  7.3 6.9 reshape.188
  19.7 7.4 convolution_bitcast_fusion
  31.5 3.5 copy.41
  35.0 8.1 squeeze.14
  43.2 5.7 reshape.194
  48.9 5.6 copy.44
  54.5 3.7 add_convert_fusion
  65.3 3.5 copy.40
  68.9 8.1 squeeze.13
  80.2 8.9 convert_bitcast_fusion.1
  92.1 5.9 reshape.183
  98.0 5.7 fusion.37
  104.5 4.0 reshape.185
  108.5 146.6 %all-reduce.8.cloned.1.call-done = f32[1970,768]{1,0:T(8,128)} async-done(((f32[1970,768]{1,0:T(8,128)}), f32[1970,768]{1,0:T(8,128)}) %all-reduce.8.cloned.1.call-update) | async-done | bytes 6051856 | tf_op jit(solution)/shard_map/psum | solution.py:93
  255.1 5.2 fusion.35
  261.3 8.0 multiply_convert_fusion.1
  269.4 9.3 convert_reduce_fusion
  281.2 6.8 fusion.39
  288.1 10.1 fusion.29
  298.2 8.9 fusion.32
  307.1 130.0 %all-reduce.10.cloned.1.call-done = f32[1970,768]{1,0:T(8,128)} async-done(((f32[1970,768]{1,0:T(8,128)}), f32[1970,768]{1,0:T(8,128)}) %all-reduce.10.cloned.1.call-update) | async-done | bytes 6051856 | tf_op jit(solution)/shard_map/psum | solution.py:125
  437.2 6.0 multiply_reduce_fusion.3
  444.3 5.8 fusion.34
  454.9 4.1 reshape.195
  459.0 4.9 copy.49
  464.0 8.5 convert_reduce_fusion.2
  472.5 12.1 %multiply_reduce_fusion = (f32[10,6,197]{2,1,0:T(8,128)S(1)}, f32[10,6,197,197]{2,3,1,0:T(8,128)}) fusion(f32[10,6,197,197]{2,3,1,0:T(8,128)} %copy-done.2, f32[10,6,197]{2,1,0:T(8,128)S(1)} %log_add_fusion, bf16[10,197,6,64]{1,3,2,0:T(8,128)(2,1)S(1)} %copy.49, bf16[10,197,6,64]{1,0,3,2:T(8,128)(2,1)} %copy-done.11), kind=kOutput, calls=%fused_computation.2 | convolution fusion | flops 307355456 | bytes 21748800 | tf_op jit(solution)/shard_map/ishd,ithd->ihst/dot_general | solution.py:146
  484.6 6.5 multiply_convert_fusion
  491.1 5.1 fusion.9
  498.9 5.8 copy.70
  504.6 6.0 reshape.193
  510.6 5.9 copy.69
  516.5 6.0 reshape.192
  522.5 4.3 copy.68
  526.9 6.1 reshape.191
  538.6 9.1 convolution_bitcast_fusion.2
  547.8 11.2 fusion.38
  559.0 6.2 convolution_bitcast_fusion.1
  567.7 236.9 %all-reduce.12.cloned.1.call-done = (f32[3,768,384]{1,2,0:T(8,128)}, f32[384,768]{1,0:T(8,128)}, f32[768,1536]{1,0:T(8,128)}, f32[1536,768]{1,0:T(8,128)}) async-done(((f32[3,768,384]{1,2,0:T(8,128)}, f32[384,768]{1,0:T(8,128)}, f32[768,1536]{1,0:T(8,128)}, f32[1536,768]{1,0:T(8,128)}), (f32[3,768,384]{1,2,0:T(8,128)}, f32[384,768]{1,0:T(8,128)}, f32[768,1536]{1,0:T(8,128)}, ...) | async-done | bytes 14155792 | tf_op jit(solution)/shard_map/psum | solution.py:190
  804.6 5.2 copy.63
  809.7 275.8 %all-reduce.14.cloned.1.call-done = (f32[1970,768]{1,0:T(8,128)}, f32[1970,768]{1,0:T(8,128)}) async-done(((f32[1970,768]{1,0:T(8,128)}, f32[1970,768]{1,0:T(8,128)}), (f32[1970,768]{1,0:T(8,128)}, f32[1970,768]{1,0:T(8,128)})) %all-reduce.14.cloned.1.call-update) | async-done | bytes 12103696 | tf_op jit(solution)/shard_map/psum | solution.py:102
  1085.6 5.9 multiply_reduce_fusion.4
  1091.8 6.7 add_convert_fusion.2
  1098.5 4.1 reshape.187
  1102.6 6.6 select_convert_fusion
  1109.1 4.1 reshape.184
  1113.3 61.7 %all-reduce = (f32[768]{0:T(1024)}, f32[768]{0:T(1024)}, f32[2,384]{1,0:T(2,128)}, f32[768]{0:T(1024)}, f32[768]{0:T(1024)}, /*index=5*/f32[768]{0:T(1024)}, f32[1536]{0:T(1024)}, f32[768]{0:T(1024)}) all-reduce(f32[768]{0:T(1024)S(1)} %get-tuple-element.44, ...), channel_id=1, replica_groups=mesh['dp'=16,'tensor'=2] {'dp'}, use_global_device_ids=true, to_apply=%region_16.17 | all-reduce | flops 6912 | bytes 55296 | tf_op jit(solution)/shard_map/psum | solution.py:190
  1176.0 5.0 copy.102
  (133 shorter events, 46.9 us)
Async XLA Ops:
  7.2 254.1 %copy-start = (bf16[768,1536]{1,0:T(8,128)(2,1)S(1)}, bf16[768,1536]{1,0:T(8,128)(2,1)}, u32[]{:S(2)}) copy-start(bf16[768,1536]{1,0:T(8,128)(2,1)} %param.25) | copy-start | bytes 7077892
  7.2 12.5 %copy-start.24 = (f32[768]{0:T(1024)S(1)}, f32[768]{0:T(1024)}, u32[]{:S(2)}) copy-start(f32[768]{0:T(1024)} %param.17) | copy-start | bytes 9220
  7.2 12.5 %copy-start.34 = (f32[768]{0:T(1024)S(1)}, f32[768]{0:T(1024)}, u32[]{:S(2)}) copy-start(f32[768]{0:T(1024)} %param.18) | copy-start | bytes 9220
  7.2 247.9 %all-reduce.8.cloned.1.call-start = ((), (), s32[]{:S(2)}) async-start(), calls=%async_computation | async-start | bytes 12140544 | tf_op jit(solution)/shard_map/psum | solution.py:93
  19.5 7.6 copy-start.20
  19.7 7.5 copy-start.22
  35.0 8.1 copy-start.29
  54.5 3.7 copy-start.5
  58.3 2.6 copy-start.10
  60.9 4.3 copy-start.2
  80.1 8.9 copy-start.11
  89.0 9.0 copy-start.16
  103.7 151.4 %copy-start.27 = (f32[768]{0:T(1024)S(1)}, f32[768]{0:T(1024)}, u32[]{:S(2)}) copy-start(f32[768]{0:T(1024)} %param.22) | copy-start | bytes 9220
  103.8 333.4 %all-reduce.10.cloned.1.call-start = ((), (), s32[]{:S(2)}) async-start(), calls=%async_computation.1 | async-start | bytes 12140544 | tf_op jit(solution)/shard_map/psum | solution.py:125
  260.4 9.0 copy-start.3
  260.4 0.9 copy-start.26
  260.4 0.9 copy-start.32
  260.4 0.9 copy-start.33
  261.3 8.1 copy-start.13
  261.3 8.1 copy-start.30
  278.7 2.6 copy-start.36
  288.0 516.6 %all-reduce.12.cloned.1.call-start = ((), (), s32[]{:S(2)}) async-start(), calls=%async_computation.2 | async-start | bytes 28311552 | tf_op jit(solution)/shard_map/psum | solution.py:190
  288.1 10.2 copy-start.37
  437.2 6.2 copy-start.8
  437.2 7.1 copy-start.14
  444.3 5.8 copy-start.9
  450.1 3.0 copy-start.4
  463.9 20.6 %slice-start = ((s8[12288000]{0:T(1024)(128)(4,1)}), s8[4194304]{0:T(1024)(128)(4,1)S(1)}, s32[]{:S(2)}) async-start(s8[12288000]{0:T(1024)(128)(4,1)} %bitcast.49), calls=%async_computation.4 | async-start | bytes 8388608
  464.0 20.6 %slice-start.1 = ((s8[12288000]{0:T(1024)(128)(4,1)}), s8[4194304]{0:T(1024)(128)(4,1)S(1)}, s32[]{:S(2)}) async-start(s8[12288000]{0:T(1024)(128)(4,1)} %bitcast.49), calls=%async_computation.5 | async-start | bytes 8388608
  472.5 12.1 %slice-start.2 = ((s8[12288000]{0:T(1024)(128)(4,1)}), s8[3899392]{0:T(1024)(128)(4,1)S(1)}, s32[]{:S(2)}) async-start(s8[12288000]{0:T(1024)(128)(4,1)} %bitcast.49), calls=%async_computation.6 | async-start | bytes 7798784
  491.1 5.1 copy-start.6
  510.6 11.9 %copy-start.12 = (bf16[10,197,6,64]{1,3,2,0:T(8,128)(2,1)S(1)}, bf16[10,197,6,64]{1,3,2,0:T(8,128)(2,1)}, u32[]{:S(2)}) copy-start(bf16[10,197,6,64]{1,3,2,0:T(8,128)(2,1)} %get-tuple-element.81) | copy-start | bytes 4538884
  526.8 9.3 copy-start.15
  526.8 11.8 copy-start.21
  526.8 11.8 copy-start.23
  526.8 11.8 copy-start.25
  526.8 11.8 copy-start.35
  536.5 2.1 copy-start.18
  547.8 537.8 %all-reduce.14.cloned.1.call-start = ((), (), s32[]{:S(2)}) async-start(), calls=%async_computation.3 | async-start | bytes 24281088 | tf_op jit(solution)/shard_map/psum | solution.py:102
  547.8 11.2 copy-start.19
  547.8 11.2 copy-start.31
  1085.6 6.2 copy-start.7
  1098.5 4.1 copy-start.28
  1109.1 65.9 %copy-start.17 = (f32[384,768]{1,0:T(8,128)S(1)}, f32[384,768]{1,0:T(8,128)}, u32[]{:S(2)}) copy-start(f32[384,768]{1,0:T(8,128)} %get-tuple-element.92) | copy-start | bytes 3538948
  1113.3 67.8 %slice-start.3 = ((s8[4718592]{0:T(1024)(128)(4,1)}), s8[524288]{0:T(1024)(128)(4,1)S(1)}, s32[]{:S(2)}) async-start(s8[4718592]{0:T(1024)(128)(4,1)} %bitcast.51), calls=%async_computation.7 | async-start | bytes 1048576
  1176.0 5.0 slice-start.4
  1176.0 7.2 copy-start.1
Sparse Core Ops, SparseCore 0:
  103.9 151.1 all-reduce.7
  288.2 148.9 all-reduce.9
  547.9 256.6 all-reduce.11
  806.9 278.5 all-reduce.13
where the time goes:
time: 1200 us; the launch traced here: 1190 us
  waiting for transfers between devices  789 us (66%)
  local copies, waits for them, and re-layouts  135 us (11%)
  matrix products  127 us (11%)
  blocking collectives  61.7 us (5%)
  other arithmetic  61 us (5%)
  between operations  15.2 us (1%)
    psum x1, waiting for transfers between devices, shards(): mlp_full = lax.psum(mlp_part, 'tensor')  276 us
    psum x1, waiting for transfers between devices, shards(): lax.psum((first_norm_gain_gradient, grad_ln1_bias, grad_w_qkv, grad_qv_bi...  237 us
    psum x1, waiting for transfers between devices, shards(): attn_full = lax.psum(attn_part, 'tensor')  147 us
    psum x1, waiting for transfers between devices, shards(): second_normed_gradient = lax.psum(norm_two_part, 'tensor')  130 us
    psum x1, blocking collectives, shards(): lax.psum((first_norm_gain_gradient, grad_ln1_bias, grad_w_qkv, grad_qv_bi...  61.7 us
    another operation x7, local copies, waits for them, and re-layouts, shards(): jnp.stack([grad_queries, grad_keys, grad_values])  34.4 us
    unnamed x92, local copies, waits for them, and re-layouts  24.3 us
  transfers between devices with their start and end apart: 4, of which 4 were waited for; matrix products, arithmetic and copies ran while one was open for 4% of the time, Pallas kernels for 0%

commit v1 on v0

--- a/solution.py
+++ b/solution.py
@@ -99,7 +99,7 @@
     pre_act = jnp.dot(normed_two_b, w_fc1, preferred_element_type=float_thirtytwo) + b_fc1
     activated = gelu_value(pre_act).astype(bfloat_sixteen)
     mlp_part = jnp.dot(activated, w_fc2, preferred_element_type=float_thirtytwo)
-    mlp_full = lax.psum(mlp_part, "tensor")
+    mlp_full = lax.all_gather(mlp_part, "tensor").sum(axis=0)
     outputs = residual_stream + (mlp_full + b_fc2)
     block_out = (
         jnp.where(live_rows, outputs, 0.0)

time: 1200 us -> 1130 us (0.942)
  waiting for transfers between devices: 789 us -> 719 us
    psum x1, waiting for transfers between devices: 276 us -> 111 us  [shards(): first_normed_gradient = lax.psum(norm_one_part, 'tensor')]
    all_gather x0 -> x1, waiting for transfers between devices: none -> 144 us  [shards(): mlp_full = lax.all_gather(mlp_part, 'tensor').sum(axis=0)]
    psum x1, waiting for transfers between devices: 237 us -> 181 us  [shards(): lax.psum((first_norm_gain_gradient, grad_ln1_bias, grad_w_qkv, grad_qv_bi...]
    unnamed x92 -> x98, local copies, waits for them, and re-layouts: 24.3 us -> 26.4 us
  transfers between devices with their start and end apart: 4 -> 5, of which waited for: 4 -> 5; matrix products, arithmetic and copies ran while one was open for 4% -> 7% of each run, Pallas kernels for 0% -> 0%
where the time goes in v1:
time: 1130 us
  waiting for transfers between devices  719 us (64%)
  local copies, waits for them, and re-layouts  137 us (12%)
  matrix products  120 us (11%)
  other arithmetic  69.2 us (6%)
  blocking collectives  65.1 us (6%)
  between operations  15.5 us (1%)
    psum x1, waiting for transfers between devices, shards(): lax.psum((first_norm_gain_gradient, grad_ln1_bias, grad_w_qkv, grad_qv_bi...  181 us
    psum x1, waiting for transfers between devices, shards(): attn_full = lax.psum(attn_part, 'tensor')  146 us
    all_gather x1, waiting for transfers between devices, shards(): mlp_full = lax.all_gather(mlp_part, 'tensor').sum(axis=0)  144 us
    psum x1, waiting for transfers between devices, shards(): second_normed_gradient = lax.psum(norm_two_part, 'tensor')  138 us
    psum x1, waiting for transfers between devices, shards(): first_normed_gradient = lax.psum(norm_one_part, 'tensor')  111 us
    psum x1, blocking collectives, shards(): lax.psum((first_norm_gain_gradient, grad_ln1_bias, grad_w_qkv, grad_qv_bi...  65.1 us
    another operation x7, local copies, waits for them, and re-layouts, shards(): jnp.stack([grad_queries, grad_keys, grad_values])  34.1 us
    unnamed x98, local copies, waits for them, and re-layouts  26.4 us
  transfers between devices with their start and end apart: 5, of which 5 were waited for; matrix products, arithmetic and copies ran while one was open for 7% of the time, Pallas kernels for 0%

profile of v1, /device:TPU:0, one launch (start us, length us, event | category | flops | bytes accessed | tf_op | source)
XLA Modules:
  0.0 1126.0 jit_solution(15803106053272681122)
XLA Ops:
  12.8 6.7 reshape.188
  19.7 7.4 convolution_bitcast_fusion
  31.6 3.5 copy.65
  35.2 5.7 reshape.198
  40.9 5.6 copy.68
  46.5 8.1 squeeze.14
  54.7 3.5 copy.64
  58.2 8.1 squeeze.13
  75.3 4.3 add_convert_fusion.1
  86.0 5.8 reshape.183
  91.7 5.7 fusion.37
  98.2 4.3 reshape.185
  102.5 146.4 %all-reduce.7.cloned.1.call-done = f32[1970,768]{1,0:T(8,128)} async-done(((f32[1970,768]{1,0:T(8,128)}), f32[1970,768]{1,0:T(8,128)}) %all-reduce.7.cloned.1.call-update) | async-done | bytes 6051856 | tf_op jit(solution)/shard_map/psum | solution.py:93
  248.8 5.2 fusion.35
  255.1 8.0 multiply_convert_fusion.1
  263.1 9.3 convert_reduce_fusion
  275.0 6.7 fusion.38
  283.4 9.4 convolution_bitcast_fusion.2
  292.9 138.0 %all-reduce.9.cloned.1.call-done = f32[1970,768]{1,0:T(8,128)} async-done(((f32[1970,768]{1,0:T(8,128)}), f32[1970,768]{1,0:T(8,128)}) %all-reduce.9.cloned.1.call-update) | async-done | bytes 6051856 | tf_op jit(solution)/shard_map/psum | solution.py:125
  430.9 6.2 multiply_reduce_fusion.3
  437.1 143.5 %all-gather.4.cloned.1.call-done = f32[2,1970,768]{2,1,0:T(8,128)} async-done(((f32[1,1970,768]{2,1,0:T(8,128)}), f32[2,1970,768]{2,1,0:T(8,128)}) %all-gather.4.cloned.1.call-update) | async-done | bytes 12103696 | tf_op jit(solution)/shard_map/all_gather | solution.py:102
  580.7 8.5 reduce_sum.185
  589.2 10.4 fusion.34
  603.9 4.1 reshape.199
  608.0 4.5 copy.73
  612.5 8.6 convert_reduce_fusion.2
  621.1 12.2 %multiply_reduce_fusion = (f32[10,6,197]{2,1,0:T(8,128)S(1)}, f32[10,6,197,197]{2,3,1,0:T(8,128)}) fusion(f32[10,6,197,197]{2,3,1,0:T(8,128)} %copy-done.2, f32[10,6,197]{2,1,0:T(8,128)S(1)} %log_add_fusion, bf16[10,197,6,64]{1,3,2,0:T(8,128)(2,1)S(1)} %copy.73, bf16[10,197,6,64]{1,0,3,2:T(8,128)(2,1)} %copy-done.10), kind=kOutput, calls=%fused_computation.2 | convolution fusion | flops 307355456 | bytes 21748800 | tf_op jit(solution)/shard_map/ishd,ithd->ihst/dot_general | solution.py:146
  633.4 6.5 multiply_convert_fusion
  639.9 5.1 fusion.9
  647.6 5.8 copy.94
  653.4 6.0 reshape.197
  659.4 5.9 copy.93
  665.3 6.0 reshape.196
  671.3 4.1 copy.92
  675.4 6.1 reshape.195
  687.3 6.2 convolution_bitcast_fusion.1
  693.6 9.9 fusion.29
  703.5 12.3 %fusion.32 = f32[768,1536]{1,0:T(8,128)} fusion(bf16[1970,1536]{1,0:T(8,128)(2,1)} %copy-done.34, f32[1970,768]{1,0:T(8,128)} %copy-done.4, f32[768]{0:T(1024)S(1)} %copy-done.31, f32[768]{0:T(1024)S(1)} %copy-done.21, f32[1970]{0:T(1024)S(1)} %add_rsqrt_fusion.1, f32[1970]{0:T(1024)S(1)} %broadcast_multiply_fusion.5), kind=kOutput, calls=%fused_computation.94 | convolution fusion | flops 4655377920 | bytes 16844176 | tf_op jit(solution)/shard_map/nd,nf->df/dot_general | solution.py:120
  718.4 6.4 convolution_bitcast_fusion.3
  727.3 4.1 reshape.184
  731.5 110.6 %all-reduce.11.cloned.1.call-done = f32[1970,768]{1,0:T(8,128)} async-done(((f32[1970,768]{1,0:T(8,128)}), f32[1970,768]{1,0:T(8,128)}) %all-reduce.11.cloned.1.call-update) | async-done | bytes 6051856 | tf_op jit(solution)/shard_map/psum | solution.py:174
  842.1 6.2 multiply_reduce_fusion.4
  848.4 6.8 add_convert_fusion.2
  855.2 4.0 reshape.187
  859.2 65.1 %all-reduce = (f32[768]{0:T(1024)}, f32[768]{0:T(1024)}, f32[2,384]{1,0:T(2,128)}, f32[768]{0:T(1024)}, f32[768]{0:T(1024)}, /*index=5*/f32[768]{0:T(1024)}, f32[1536]{0:T(1024)}, f32[768]{0:T(1024)}) all-reduce(f32[768]{0:T(1024)S(1)} %get-tuple-element.58, ...), channel_id=1, replica_groups=mesh['dp'=16,'tensor'=2] {'dp'}, use_global_device_ids=true, to_apply=%region_16.17 | all-reduce | flops 6912 | bytes 55296 | tf_op jit(solution)/shard_map/psum | solution.py:190
  924.3 180.8 %all-reduce.13.cloned.1.call-done = (f32[3,768,384]{1,2,0:T(8,128)}, f32[384,768]{1,0:T(8,128)}, f32[768,1536]{1,0:T(8,128)}, f32[1536,768]{1,0:T(8,128)}) async-done(((f32[3,768,384]{1,2,0:T(8,128)}, f32[384,768]{1,0:T(8,128)}, f32[768,1536]{1,0:T(8,128)}, f32[1536,768]{1,0:T(8,128)}), (f32[3,768,384]{1,2,0:T(8,128)}, f32[384,768]{1,0:T(8,128)}, f32[768,1536]{1,0:T(8,128)}, ...) | async-done | bytes 14155792 | tf_op jit(solution)/shard_map/psum | solution.py:190
  1105.1 5.2 copy.87
  1111.3 5.5 copy.125
  (145 shorter events, 51.7 us)
Async XLA Ops:
  7.2 247.8 %copy-start = (bf16[768,1536]{1,0:T(8,128)(2,1)S(1)}, bf16[768,1536]{1,0:T(8,128)(2,1)}, u32[]{:S(2)}) copy-start(bf16[768,1536]{1,0:T(8,128)(2,1)} %param.25) | copy-start | bytes 7077892
  7.2 241.6 %all-reduce.7.cloned.1.call-start = ((), (), s32[]{:S(2)}) async-start(), calls=%async_computation | async-start | bytes 12140544 | tf_op jit(solution)/shard_map/psum | solution.py:93
  9.9 9.8 copy-start.17
  9.9 9.8 copy-start.22
  9.9 9.8 copy-start.32
  19.7 7.5 copy-start.19
  28.4 3.0 copy-start.26
  66.3 3.5 copy-start.5
  69.8 2.6 copy-start.9
  72.4 7.3 copy-start.2
  79.7 3.2 copy-start.10
  83.0 8.8 copy-start.14
  97.5 151.4 %copy-start.24 = (f32[768]{0:T(1024)S(1)}, f32[768]{0:T(1024)}, u32[]{:S(2)}) copy-start(f32[768]{0:T(1024)} %param.22) | copy-start | bytes 9220
  97.5 333.4 %all-reduce.9.cloned.1.call-start = ((), (), s32[]{:S(2)}) async-start(), calls=%async_computation.1 | async-start | bytes 12140544 | tf_op jit(solution)/shard_map/psum | solution.py:125
  254.1 9.0 copy-start.4
  255.0 8.1 copy-start.12
  255.0 8.1 copy-start.27
  272.4 2.6 copy-start.34
  281.7 1.7 copy-start.28
  281.8 298.9 %all-gather.4.cloned.1.call-start = ((), (), s32[]{:S(2)}) async-start(), calls=%async_computation.3 | async-start | bytes 18210816 | tf_op jit(solution)/shard_map/all_gather | solution.py:102
  292.8 549.3 %all-reduce.11.cloned.1.call-start = ((), (), s32[]{:S(2)}) async-start(), calls=%async_computation.2 | async-start | bytes 12140544 | tf_op jit(solution)/shard_map/psum | solution.py:174
  437.1 152.0 %copy-start.25 = (f32[768]{0:T(1024)S(1)}, f32[768]{0:T(1024)}, u32[]{:S(2)}) copy-start(f32[768]{0:T(1024)} %param.28) | copy-start | bytes 9220
  599.6 2.5 copy-start.3
  612.5 20.8 %slice-start = ((s8[12288000]{0:T(1024)(128)(4,1)}), s8[4194304]{0:T(1024)(128)(4,1)S(1)}, s32[]{:S(2)}) async-start(s8[12288000]{0:T(1024)(128)(4,1)} %bitcast.51), calls=%async_computation.5 | async-start | bytes 8388608
  612.5 20.8 %slice-start.1 = ((s8[12288000]{0:T(1024)(128)(4,1)}), s8[4194304]{0:T(1024)(128)(4,1)S(1)}, s32[]{:S(2)}) async-start(s8[12288000]{0:T(1024)(128)(4,1)} %bitcast.51), calls=%async_computation.6 | async-start | bytes 8388608
  621.1 12.3 %slice-start.2 = ((s8[12288000]{0:T(1024)(128)(4,1)}), s8[3899392]{0:T(1024)(128)(4,1)S(1)}, s32[]{:S(2)}) async-start(s8[12288000]{0:T(1024)(128)(4,1)} %bitcast.51), calls=%async_computation.7 | async-start | bytes 7798784
  639.9 5.1 copy-start.6
  659.4 11.9 %copy-start.11 = (bf16[10,197,6,64]{1,3,2,0:T(8,128)(2,1)S(1)}, bf16[10,197,6,64]{1,3,2,0:T(8,128)(2,1)}, u32[]{:S(2)}) copy-start(bf16[10,197,6,64]{1,3,2,0:T(8,128)(2,1)} %get-tuple-element.94) | copy-start | bytes 4538884
  675.4 9.5 copy-start.13
  681.5 5.8 copy-start.29
  685.2 2.1 copy-start.16
  693.5 411.6 %all-reduce.13.cloned.1.call-start = ((), (), s32[]{:S(2)}) async-start(), calls=%async_computation.4 | async-start | bytes 28311552 | tf_op jit(solution)/shard_map/psum | solution.py:190
  693.6 22.3 %slice-start.3 = ((s8[6070272]{0:T(1024)(128)(4,1)}), s8[4194304]{0:T(1024)(128)(4,1)S(1)}, s32[]{:S(2)}) async-start(s8[6070272]{0:T(1024)(128)(4,1)} %bitcast.53), calls=%async_computation.8 | async-start | bytes 8388608
  693.6 24.8 %slice-start.5 = ((s8[6070272]{0:T(1024)(128)(4,1)}), s8[4194304]{0:T(1024)(128)(4,1)S(1)}, s32[]{:S(2)}) async-start(s8[6070272]{0:T(1024)(128)(4,1)} %bitcast.55), calls=%async_computation.10 | async-start | bytes 8388608
  693.6 24.8 %slice-start.9 = ((s8[4552704]{0:T(1024)(128)(4,1)}), s8[4194304]{0:T(1024)(128)(4,1)S(1)}, s32[]{:S(2)}) async-start(s8[4552704]{0:T(1024)(128)(4,1)} %bitcast.59), calls=%async_computation.14 | async-start | bytes 8388608
  703.5 12.4 %slice-start.4 = ((s8[6070272]{0:T(1024)(128)(4,1)}), s8[1875968]{0:T(1024)(128)(4,1)S(1)}, s32[]{:S(2)}) async-start(s8[6070272]{0:T(1024)(128)(4,1)} %bitcast.53), calls=%async_computation.9 | async-start | bytes 3751936
  703.5 12.4 %copy-start.8 = (bf16[1970,384]{0,1:T(8,128)(2,1)S(1)}, bf16[1970,384]{0,1:T(8,128)(2,1)}, u32[]{:S(2)}) copy-start(bf16[1970,384]{0,1:T(8,128)(2,1)} %reshape.183) | copy-start | bytes 4538884
  703.5 14.8 %slice-start.6 = ((s8[6070272]{0:T(1024)(128)(4,1)}), s8[1875968]{0:T(1024)(128)(4,1)S(1)}, s32[]{:S(2)}) async-start(s8[6070272]{0:T(1024)(128)(4,1)} %bitcast.55), calls=%async_computation.11 | async-start | bytes 3751936
  703.5 14.8 %slice-start.10 = ((s8[4552704]{0:T(1024)(128)(4,1)}), s8[358400]{0:T(1024)(128)(4,1)S(1)}, s32[]{:S(2)}) async-start(s8[4552704]{0:T(1024)(128)(4,1)} %bitcast.59), calls=%async_computation.15 | async-start | bytes 716800
  715.9 2.5 copy-start.18
  715.9 2.5 copy-start.20
  715.9 2.5 copy-start.23
  715.9 2.5 copy-start.33
  842.1 6.2 copy-start.7
  1105.1 5.3 copy-start.15
  1110.3 6.5 slice-start.7
  1111.3 5.5 slice-start.8
  1111.3 7.7 copy-start.1
  (3 other events, 2.8 us)
Sparse Core Ops, SparseCore 0:
  97.6 151.1 all-reduce.6
  281.9 148.9 all-reduce.8
  432.5 148.1 all-gather.3
  693.6 148.4 all-reduce.10
  847.7 257.3 all-reduce.12
